TPU v7x, 512 devices: a whole 4x8x8 slice. The times are simulated.
512 devices in a mesh: tile: 64 (over y, z_hi, core), layer: 8 (over x, z_lo).
Axes of the slice: x: 4, y: 8, z: 8 (z_hi: 4, z_lo: 2; z = z_hi * 2 + z_lo), core: 2. Of those that a mesh axis runs over, the one named last changes fastest.
Arguments:
- class_index: int32 [8, 2, 1024, 8192], P('layer', None, 'tile'), may hold values from 0 to 15
- class_conductance: float32 [8, 16], P('layer'), may hold values from 0.5 to 8
- loads: float32 [8, 1024, 8192], P('layer', 'tile'), may hold values from -4 to 4
- start_volts: float32 [8, 1024, 8192], P('layer', 'tile'), may hold values from 0.8 to 1
- via_cells: int32 [8, 524288], P('layer', 'tile'), may hold values from 0 to 15, as said below
- via_counts: int32 [8, 524288], P('layer', 'tile'), may hold values from 0 to 4
Outputs:
- volts: float32 [8, 1024, 8192], P('layer', 'tile')
Inputs may be any that keep to these rules, and one draw needn't show every extreme that they name: `via_cells`: each slot names a row of its own strip; slot s sits in column s % 8192, so each column of a strip holds exactly one slot of each layer.
All inputs are finite; a program needn't handle non-finite values.
Results may differ from a plain program's by a relative error of at most 0.00002.
Values sent between devices are 32-bit elements; how exact they have to be, the bound alone decides.
A program may use at most 64 MiB of HBM per device.

v0:
```python
import jax
import jax.numpy as jnp
from jax import lax
from jax.sharding import PartitionSpec as P

CLASSES = 16
OUTER = 2
SWEEPS = 3


VIA_UNIT = 2.0
LOWER_BOUND = 0.05
UPPER_BOUND = 2.0


def passed_along(block, axis, distance):
    devices = range(lax.axis_size(axis))
    route = [(i - distance, i) for i in devices if i - distance in devices]
    return lax.ppermute(block, axis, route)


def padded_2(shard, sides, width):
    for axis, dim in sides:
        peers, length = (lax.axis_size(axis), shard.shape[dim])
        up = [(i, (i + 1) % peers) for i in range(peers - 1)]
        down = [(j, i) for i, j in up]
        last = lax.slice_in_dim(shard, length - width, length, axis=dim)
        leading = lax.slice_in_dim(shard, 0, width, axis=dim)
        before = lax.ppermute(last, axis, up)
        after = lax.ppermute(leading, axis, down)
        shard = jnp.concatenate([before, shard, after], axis=dim)
    return shard


def chebyshev_terms(count):
    centre_value = 0.5 * (UPPER_BOUND + LOWER_BOUND)
    half_width = 0.5 * (UPPER_BOUND - LOWER_BOUND)
    sigma = centre_value / half_width
    rho_last = 1.0 / sigma
    terms = [(0.0, 1.0 / centre_value)]
    for index in range(1, count):
        rho_next = 1.0 / (2.0 * sigma - rho_last)
        terms.append((rho_next * rho_last, 2.0 * rho_next / half_width))
        rho_last = rho_next
    return terms


def lookup(class_codes, class_table):
    result = jnp.zeros(class_codes.shape, jnp.float32)
    for code in range(CLASSES):
        result = result + jnp.where(class_codes == code, class_table[code], jnp.float32(0.0))
    return result


def neighbours(padded, vertical_links, across):
    span = padded.shape[0]
    centre_cells = padded[1 : span - 1]
    vertical = (
        vertical_links[0 : span - 2] * padded[0 : span - 2]
        + vertical_links[1 : span - 1] * padded[2:span]
    )
    right_flow = jnp.pad(centre_cells[:, 1:], ((0, 0), (0, 1))) * across
    left_flow = jnp.pad(centre_cells[:, :-1] * across[:, :-1], ((0, 0), (1, 0)))
    return vertical + right_flow + left_flow


def relax_sweep(padded, vertical_links, across, right_side, inverse_diag, previous, factors):
    centre_cells = padded[1:-1]
    residual = (
        inverse_diag * (right_side + neighbours(padded, vertical_links, across)) - centre_cells
    )
    if previous is None:
        update = factors[1] * residual
    else:
        update = factors[0] * previous + factors[1] * residual
    return (centre_cells + update, update)


def pick_rows(field, marks):
    return jnp.sum(jnp.where(marks, field, jnp.float32(0.0)), axis=0)


def local(class_index, class_conductance, loads, start_volts, via_cells, via_counts):
    row_count = loads.shape[1]
    col_count = loads.shape[2]
    conductance = lookup(class_index[0], class_conductance[0])
    col_ids = lax.broadcasted_iota(jnp.int32, (row_count, col_count), 1)
    local_rows = lax.broadcasted_iota(jnp.int32, (row_count, col_count), 0)
    row_ids = local_rows + lax.axis_index("tile") * row_count
    across = jnp.where(col_ids < col_count - 1, conductance[0], jnp.float32(0.0))
    downward = jnp.where(
        row_ids < lax.axis_size("tile") * row_count - 1, conductance[1], jnp.float32(0.0)
    )
    upper_links = passed_along(downward[row_count - 1 :], "tile", 1)
    vertical_links = jnp.concatenate([upper_links, downward], axis=0)
    own_cells = via_cells[0]
    own_counts = via_counts[0]
    lower_cells, lower_counts = passed_along((own_cells, own_counts), "layer", 1)
    own_weight = VIA_UNIT * own_counts.astype(jnp.float32)
    lower_weight = VIA_UNIT * lower_counts.astype(jnp.float32)
    own_marks = local_rows == own_cells[None, :]
    lower_marks = local_rows == lower_cells[None, :]
    zero_value = jnp.float32(0.0)
    via_diag = jnp.where(own_marks, own_weight[None, :], zero_value) + jnp.where(
        lower_marks, lower_weight[None, :], zero_value
    )
    diagonal = (
        across
        + jnp.pad(across[:, :-1], ((0, 0), (1, 0)))
        + vertical_links[:-1]
        + vertical_links[1:]
        + via_diag
    )
    inverse_diag = 1.0 / diagonal
    on_top_layer = lax.axis_index("layer") == lax.axis_size("layer") - 1
    factors = chebyshev_terms(SWEEPS)
    volts = start_volts[0]
    for outer_index in range(OUTER):
        from_below = passed_along(pick_rows(volts, own_marks), "layer", 1)
        from_above = passed_along(pick_rows(volts, lower_marks), "layer", -1)
        from_above = jnp.where(on_top_layer, jnp.float32(1.0), from_above)
        source = jnp.where(own_marks, (own_weight * from_above)[None, :], zero_value) + jnp.where(
            lower_marks, (lower_weight * from_below)[None, :], zero_value
        )
        right_side = source - loads[0]
        update = None
        for sweep_index in range(SWEEPS):
            padded = padded_2(volts, (("tile", 0),), 1)
            volts, update = relax_sweep(
                padded,
                vertical_links,
                across,
                right_side,
                inverse_diag,
                update,
                factors[sweep_index],
            )
    return volts[None]


def solution(mesh):
    placed = (
        P("layer", None, "tile", None),
        P("layer", None),
        P("layer", "tile", None),
        P("layer", "tile", None),
        P("layer", "tile"),
        P("layer", "tile"),
    )
    return jax.shard_map(
        local, mesh=mesh, in_specs=placed, out_specs=P("layer", "tile", None), check_vma=False
    )
```

profile of v0, /device:TPU:96, one launch (start us, length us, event | category | flops | bytes accessed | tf_op | source)
XLA Modules:
  0.0 117.5 jit_solution(14988510466240939983)
XLA Ops:
  0.0 2.5 %collective-permute-start.1 = (s32[8192]{0:T(1024)}, s32[8192]{0:T(1024)S(1)}, u32[]{:S(2)}, u32[]{:S(2)}) collective-permute-start(s32[8192]{0:T(1024)} %bitcast.64), channel_id=1, source_target_pairs={{0,1},{1,2},{2,3},{3,4},{4,5},{5,6},{6,7},{8,9},{9,10},{10,11},{11... | collective-permute-start | bytes 98312 | tf_op jit(solution)/shard_map/ppermute | solution.py:19
  2.5 4.3 %collective-permute-start.2 = (s32[8192]{0:T(1024)}, s32[8192]{0:T(1024)S(1)}, u32[]{:S(2)}, u32[]{:S(2)}) collective-permute-start(s32[8192]{0:T(1024)} %bitcast.78), channel_id=1, source_target_pairs={{0,1},{1,2},{2,3},{3,4},{4,5},{5,6},{6,7},{8,9},{9,10},{10,11},{11... | collective-permute-start | bytes 98312 | tf_op jit(solution)/shard_map/ppermute | solution.py:19
  6.8 1.7 %slice_bitcast_fusion.3 = (f32[1,8192]{1,0:T(1,128)}, f32[1,8192]{1,0:T(1,128)S(1)}) fusion(f32[1,16,8192]{2,1,0:T(8,128)} %param.9), kind=kLoop, calls=%fused_computation.101 | loop fusion | bytes 131072 | tf_op jit(solution)/shard_map/slice | solution.py:27
  8.5 1.9 %collective-permute-start.5 = (f32[1,8192]{1,0:T(1,128)}, f32[1,8192]{1,0:T(1,128)S(1)}, u32[]{:S(2)}, u32[]{:S(2)}) collective-permute-start(f32[1,8192]{1,0:T(1,128)} %get-tuple-element.43), channel_id=1, source_target_pairs={{0,8},{8,16},{16,24},{24,32},{32,40},{40,48},{48,56},{56,64},{64,7... | collective-permute-start | bytes 98312 | tf_op jit(solution)/shard_map/ppermute | solution.py:29
  10.4 8.8 %collective-permute-start.6 = (f32[1,8192]{1,0:T(1,128)S(1)}, f32[1,8192]{1,0:T(1,128)S(1)}, u32[]{:S(2)}, u32[]{:S(2)}) collective-permute-start(f32[1,8192]{1,0:T(1,128)S(1)} %get-tuple-element.44), channel_id=1, source_target_pairs={{8,0},{16,8},{24,16},{32,24},{40,32},{48,40},{56,48},{64,56},{72,6... | collective-permute-start | bytes 98312 | tf_op jit(solution)/shard_map/ppermute | solution.py:30
  20.6 12.7 %bitcast_add_fusion = f32[2,16,8192]{2,1,0:T(8,128)S(1)} fusion(s32[1,2,16,8192]{3,2,1,0:T(8,128)} %param.6, f32[]{:T(128)} %bitcast.17, f32[]{:T(128)} %bitcast.15, f32[]{:T(128)} %bitcast.14, f32[]{:T(128)} %bitcast.13, f32[]{:T(128)} %bitcast.12, f32[]{:T(128)} %bitcast.11, f32[]{:T(128)} %bitcast.10, f32[]{:T(128)} %bitcast.9, f32[]{:T(128)} %bitcast.8, ...), kind=kLoop, calls=%fused_computation | loop fusion | flops 12320768 | bytes 2097216 | tf_op jit(solution)/shard_map/add | solution.py:51
  33.4 1.9 %collective-permute-start = (f32[1,8192]{1,0:T(1,128)S(1)}, f32[1,8192]{1,0:T(1,128)S(1)}, u32[]{:S(2)}, u32[]{:S(2)}) collective-permute-start(f32[1,8192]{1,0:T(1,128)S(1)} %slice.279), channel_id=1, source_target_pairs={{0,8},{8,16},{16,24},{24,32},{32,40},{40,48},{48,56},{56,64},{64,7... | collective-permute-start | bytes 98312 | tf_op jit(solution)/shard_map/ppermute | solution.py:19
  35.3 1.0 fusion.84
  36.6 3.4 %collective-permute-start.4 = (f32[8192]{0:T(1024)S(1)}, f32[8192]{0:T(1024)}, u32[]{:S(2)}, u32[]{:S(2)}) collective-permute-start(f32[8192]{0:T(1024)S(1)} %get-tuple-element.8), channel_id=1, source_target_pairs={{0,1},{1,2},{2,3},{3,4},{4,5},{5,6},{6,7},{8,9},{9,10},{10,11},{11... | collective-permute-start | bytes 98312 | tf_op jit(solution)/shard_map/ppermute | solution.py:19
  40.1 3.0 %collective-permute-start.3 = (f32[8192]{0:T(1024)S(1)}, f32[8192]{0:T(1024)S(1)}, u32[]{:S(2)}, u32[]{:S(2)}) collective-permute-start(f32[8192]{0:T(1024)S(1)} %get-tuple-element.7), channel_id=1, source_target_pairs={{1,0},{2,1},{3,2},{4,3},{5,4},{6,5},{7,6},{9,8},{10,9},{11,10},{12... | collective-permute-start | bytes 98312 | tf_op jit(solution)/shard_map/ppermute | solution.py:19
  43.9 2.9 %collective-permute-done.3 = f32[8192]{0:T(1024)S(1)} collective-permute-done((f32[8192]{0:T(1024)S(1)}, f32[8192]{0:T(1024)S(1)}, u32[]{:S(2)}, u32[]{:S(2)}) %collective-permute-start.3) | collective-permute-done | bytes 32800 | tf_op jit(solution)/shard_map/ppermute | solution.py:19
  46.8 1.7 %multiply_add_fusion.1 = (f32[16,8192]{1,0:T(8,128)S(1)}, f32[16,8192]{1,0:T(8,128)S(1)}) fusion(f32[1,16,8192]{2,1,0:T(8,128)S(1)} %copy-done, f32[16,8192]{1,0:T(8,128)S(1)} %bitcast.63, f32[16,8191]{1,0:T(8,128)S(1)} %get-tuple-element.41, f32[16,8192]{1,0:T(8,128)S(1)} %get-tuple-element.19, f32[16,8191]{1,0:T(8,128)} %get-tuple-element.42, ...), kind=kLoop, calls=%fused_computation.92 | loop fusion | flops 3670016 | bytes 5537600 | tf_op jit(solution)/shard_map/add | solution.py:76
  48.6 1.9 %collective-permute-start.7 = (f32[1,8192]{1,0:T(1,128)S(1)}, f32[1,8192]{1,0:T(1,128)S(1)}, u32[]{:S(2)}, u32[]{:S(2)}) collective-permute-start(f32[1,8192]{1,0:T(1,128)S(1)} %get-tuple-element.36), channel_id=1, source_target_pairs={{0,8},{8,16},{16,24},{24,32},{32,40},{40,48},{48,56},{56,64},{64,7... | collective-permute-start | bytes 98312 | tf_op jit(solution)/shard_map/ppermute | solution.py:29
  50.6 7.9 %collective-permute-start.8 = (f32[1,8192]{1,0:T(1,128)S(1)}, f32[1,8192]{1,0:T(1,128)S(1)}, u32[]{:S(2)}, u32[]{:S(2)}) collective-permute-start(f32[1,8192]{1,0:T(1,128)S(1)} %get-tuple-element.37), channel_id=1, source_target_pairs={{8,0},{16,8},{24,16},{32,24},{40,32},{48,40},{56,48},{64,56},{72,6... | collective-permute-start | bytes 98312 | tf_op jit(solution)/shard_map/ppermute | solution.py:30
  58.6 1.4 %collective-permute-done.8 = f32[1,8192]{1,0:T(1,128)S(1)} collective-permute-done((f32[1,8192]{1,0:T(1,128)S(1)}, f32[1,8192]{1,0:T(1,128)S(1)}, u32[]{:S(2)}, u32[]{:S(2)}) %collective-permute-start.8) | collective-permute-done | bytes 32800 | tf_op jit(solution)/shard_map/ppermute | solution.py:30
  60.8 1.9 %collective-permute-start.9 = (f32[1,8192]{1,0:T(1,128)S(1)}, f32[1,8192]{1,0:T(1,128)S(1)}, u32[]{:S(2)}, u32[]{:S(2)}) collective-permute-start(f32[1,8192]{1,0:T(1,128)S(1)} %get-tuple-element.32), channel_id=1, source_target_pairs={{0,8},{8,16},{16,24},{24,32},{32,40},{40,48},{48,56},{56,64},{64,7... | collective-permute-start | bytes 98312 | tf_op jit(solution)/shard_map/ppermute | solution.py:29
  62.8 7.9 %collective-permute-start.10 = (f32[1,8192]{1,0:T(1,128)S(1)}, f32[1,8192]{1,0:T(1,128)S(1)}, u32[]{:S(2)}, u32[]{:S(2)}) collective-permute-start(f32[1,8192]{1,0:T(1,128)S(1)} %get-tuple-element.33), channel_id=1, source_target_pairs={{8,0},{16,8},{24,16},{32,24},{40,32},{48,40},{56,48},{64,56},{72,6... | collective-permute-start | bytes 98312 | tf_op jit(solution)/shard_map/ppermute | solution.py:30
  70.9 1.4 %collective-permute-done.10 = f32[1,8192]{1,0:T(1,128)S(1)} collective-permute-done((f32[1,8192]{1,0:T(1,128)S(1)}, f32[1,8192]{1,0:T(1,128)S(1)}, u32[]{:S(2)}, u32[]{:S(2)}) %collective-permute-start.10) | collective-permute-done | bytes 32800 | tf_op jit(solution)/shard_map/ppermute | solution.py:30
  72.2 0.9 select_reduce_fusion.1
  73.1 2.1 %collective-permute-start.11 = (f32[8192]{0:T(1024)S(1)}, f32[8192]{0:T(1024)S(1)}, u32[]{:S(2)}, u32[]{:S(2)}) collective-permute-start(f32[8192]{0:T(1024)S(1)} %get-tuple-element.5), channel_id=1, source_target_pairs={{1,0},{2,1},{3,2},{4,3},{5,4},{6,5},{7,6},{9,8},{10,9},{11,10},{12... | collective-permute-start | bytes 98312 | tf_op jit(solution)/shard_map/ppermute | solution.py:19
  75.5 4.6 %collective-permute-start.12 = (f32[8192]{0:T(1024)S(1)}, f32[8192]{0:T(1024)S(1)}, u32[]{:S(2)}, u32[]{:S(2)}) collective-permute-start(f32[8192]{0:T(1024)S(1)} %get-tuple-element.6), channel_id=1, source_target_pairs={{0,1},{1,2},{2,3},{3,4},{4,5},{5,6},{6,7},{8,9},{9,10},{10,11},{11... | collective-permute-start | bytes 98312 | tf_op jit(solution)/shard_map/ppermute | solution.py:19
  80.2 1.9 %collective-permute-start.13 = (f32[1,8192]{1,0:T(1,128)S(1)}, f32[1,8192]{1,0:T(1,128)S(1)}, u32[]{:S(2)}, u32[]{:S(2)}) collective-permute-start(f32[1,8192]{1,0:T(1,128)S(1)} %get-tuple-element.28), channel_id=1, source_target_pairs={{0,8},{8,16},{16,24},{24,32},{32,40},{40,48},{48,56},{56,64},{64,7... | collective-permute-start | bytes 98312 | tf_op jit(solution)/shard_map/ppermute | solution.py:29
  82.1 7.9 %collective-permute-start.14 = (f32[1,8192]{1,0:T(1,128)S(1)}, f32[1,8192]{1,0:T(1,128)S(1)}, u32[]{:S(2)}, u32[]{:S(2)}) collective-permute-start(f32[1,8192]{1,0:T(1,128)S(1)} %get-tuple-element.29), channel_id=1, source_target_pairs={{8,0},{16,8},{24,16},{32,24},{40,32},{48,40},{56,48},{64,56},{72,6... | collective-permute-start | bytes 98312 | tf_op jit(solution)/shard_map/ppermute | solution.py:30
  90.0 1.5 %collective-permute-done.14 = f32[1,8192]{1,0:T(1,128)S(1)} collective-permute-done((f32[1,8192]{1,0:T(1,128)S(1)}, f32[1,8192]{1,0:T(1,128)S(1)}, u32[]{:S(2)}, u32[]{:S(2)}) %collective-permute-start.14) | collective-permute-done | bytes 32800 | tf_op jit(solution)/shard_map/ppermute | solution.py:30
  92.3 1.9 %collective-permute-start.15 = (f32[1,8192]{1,0:T(1,128)S(1)}, f32[1,8192]{1,0:T(1,128)S(1)}, u32[]{:S(2)}, u32[]{:S(2)}) collective-permute-start(f32[1,8192]{1,0:T(1,128)S(1)} %get-tuple-element.24), channel_id=1, source_target_pairs={{0,8},{8,16},{16,24},{24,32},{32,40},{40,48},{48,56},{56,64},{64,7... | collective-permute-start | bytes 98312 | tf_op jit(solution)/shard_map/ppermute | solution.py:29
  94.2 7.9 %collective-permute-start.16 = (f32[1,8192]{1,0:T(1,128)S(1)}, f32[1,8192]{1,0:T(1,128)S(1)}, u32[]{:S(2)}, u32[]{:S(2)}) collective-permute-start(f32[1,8192]{1,0:T(1,128)S(1)} %get-tuple-element.25), channel_id=1, source_target_pairs={{8,0},{16,8},{24,16},{32,24},{40,32},{48,40},{56,48},{64,56},{72,6... | collective-permute-start | bytes 98312 | tf_op jit(solution)/shard_map/ppermute | solution.py:30
  102.3 1.4 %collective-permute-done.16 = f32[1,8192]{1,0:T(1,128)S(1)} collective-permute-done((f32[1,8192]{1,0:T(1,128)S(1)}, f32[1,8192]{1,0:T(1,128)S(1)}, u32[]{:S(2)}, u32[]{:S(2)}) %collective-permute-start.16) | collective-permute-done | bytes 32800 | tf_op jit(solution)/shard_map/ppermute | solution.py:30
  103.7 0.8 fusion.65
  104.5 1.9 %collective-permute-start.17 = (f32[1,8192]{1,0:T(1,128)S(1)}, f32[1,8192]{1,0:T(1,128)S(1)}, u32[]{:S(2)}, u32[]{:S(2)}) collective-permute-start(f32[1,8192]{1,0:T(1,128)S(1)} %get-tuple-element.22), channel_id=1, source_target_pairs={{0,8},{8,16},{16,24},{24,32},{32,40},{40,48},{48,56},{56,64},{64,7... | collective-permute-start | bytes 98312 | tf_op jit(solution)/shard_map/ppermute | solution.py:29
  106.5 7.9 %collective-permute-start.18 = (f32[1,8192]{1,0:T(1,128)S(1)}, f32[1,8192]{1,0:T(1,128)S(1)}, u32[]{:S(2)}, u32[]{:S(2)}) collective-permute-start(f32[1,8192]{1,0:T(1,128)S(1)} %get-tuple-element.23), channel_id=1, source_target_pairs={{8,0},{16,8},{24,16},{32,24},{40,32},{48,40},{56,48},{64,56},{72,6... | collective-permute-start | bytes 98312 | tf_op jit(solution)/shard_map/ppermute | solution.py:30
  114.6 1.4 %collective-permute-done.18 = f32[1,8192]{1,0:T(1,128)S(1)} collective-permute-done((f32[1,8192]{1,0:T(1,128)S(1)}, f32[1,8192]{1,0:T(1,128)S(1)}, u32[]{:S(2)}, u32[]{:S(2)}) %collective-permute-start.18) | collective-permute-done | bytes 32800 | tf_op jit(solution)/shard_map/ppermute | solution.py:30
  115.9 1.5 %fusion.10 = f32[1,16,8192]{2,1,0:T(8,128)} fusion(f32[16,8192]{1,0:T(8,128)S(1)} %get-tuple-element.9, f32[16,8192]{1,0:T(8,128)S(1)} %get-tuple-element.18, f32[1,8192]{1,0:T(1,128)S(1)} %collective-permute-done.18, f32[1,8192]{1,0:T(1,128)S(1)} %collective-permute-done.17, f32[1,8192]{1,0:T(1,128)S(1)} %collective-permute-done, ...), kind=kLoop, calls=%fused_computation.13 | loop fusion | flops 3932160 | bytes 5013312 | tf_op jit(solution)/shard_map/broadcast_in_dim | solution.py:138
  (46 shorter events, 5.4 us)
Async XLA Ops:
  0.0 36.3 %collective-permute-start.1 = (s32[8192]{0:T(1024)}, s32[8192]{0:T(1024)S(1)}, u32[]{:S(2)}, u32[]{:S(2)}) collective-permute-start(s32[8192]{0:T(1024)} %bitcast.64), channel_id=1, source_target_pairs={{0,1},{1,2},{2,3},{3,4},{4,5},{5,6},{6,7},{8,9},{9,10},{10,11},{11... | collective-permute-start | bytes 98312 | tf_op jit(solution)/shard_map/ppermute | solution.py:19
  2.5 37.6 %collective-permute-start.2 = (s32[8192]{0:T(1024)}, s32[8192]{0:T(1024)S(1)}, u32[]{:S(2)}, u32[]{:S(2)}) collective-permute-start(s32[8192]{0:T(1024)} %bitcast.78), channel_id=1, source_target_pairs={{0,1},{1,2},{2,3},{3,4},{4,5},{5,6},{6,7},{8,9},{9,10},{10,11},{11... | collective-permute-start | bytes 98312 | tf_op jit(solution)/shard_map/ppermute | solution.py:19
  8.5 38.3 %collective-permute-start.5 = (f32[1,8192]{1,0:T(1,128)}, f32[1,8192]{1,0:T(1,128)S(1)}, u32[]{:S(2)}, u32[]{:S(2)}) collective-permute-start(f32[1,8192]{1,0:T(1,128)} %get-tuple-element.43), channel_id=1, source_target_pairs={{0,8},{8,16},{16,24},{24,32},{32,40},{40,48},{48,56},{56,64},{64,7... | collective-permute-start | bytes 98312 | tf_op jit(solution)/shard_map/ppermute | solution.py:29
  10.4 36.4 %collective-permute-start.6 = (f32[1,8192]{1,0:T(1,128)S(1)}, f32[1,8192]{1,0:T(1,128)S(1)}, u32[]{:S(2)}, u32[]{:S(2)}) collective-permute-start(f32[1,8192]{1,0:T(1,128)S(1)} %get-tuple-element.44), channel_id=1, source_target_pairs={{8,0},{16,8},{24,16},{32,24},{40,32},{48,40},{56,48},{64,56},{72,6... | collective-permute-start | bytes 98312 | tf_op jit(solution)/shard_map/ppermute | solution.py:30
  19.2 0.7 copy-start.4
  33.2 2.1 %copy-start = (f32[1,16,8192]{2,1,0:T(8,128)S(1)}, f32[1,16,8192]{2,1,0:T(8,128)}, u32[]{:S(2)}) copy-start(f32[1,16,8192]{2,1,0:T(8,128)} %param.9) | copy-start | bytes 1572868
  33.4 13.4 %collective-permute-start = (f32[1,8192]{1,0:T(1,128)S(1)}, f32[1,8192]{1,0:T(1,128)S(1)}, u32[]{:S(2)}, u32[]{:S(2)}) collective-permute-start(f32[1,8192]{1,0:T(1,128)S(1)} %slice.279), channel_id=1, source_target_pairs={{0,8},{8,16},{16,24},{24,32},{32,40},{40,48},{48,56},{56,64},{64,7... | collective-permute-start | bytes 98312 | tf_op jit(solution)/shard_map/ppermute | solution.py:19
  35.3 1.0 copy-start.2
  36.3 3.7 %copy-start.3 = (s32[1,8192]{1,0:T(1,128)S(1)}, s32[1,8192]{1,0:T(1,128)}, u32[]{:S(2)}) copy-start(s32[1,8192]{1,0:T(1,128)} %param.11) | copy-start | bytes 98308
  36.3 10.5 %copy-start.1 = (f32[1,16,8192]{2,1,0:T(8,128)S(1)}, f32[1,16,8192]{2,1,0:T(8,128)}, u32[]{:S(2)}) copy-start(f32[1,16,8192]{2,1,0:T(8,128)} %param.8) | copy-start | bytes 1572868
  36.6 6.5 %collective-permute-start.4 = (f32[8192]{0:T(1024)S(1)}, f32[8192]{0:T(1024)}, u32[]{:S(2)}, u32[]{:S(2)}) collective-permute-start(f32[8192]{0:T(1024)S(1)} %get-tuple-element.8), channel_id=1, source_target_pairs={{0,1},{1,2},{2,3},{3,4},{4,5},{5,6},{6,7},{8,9},{9,10},{10,11},{11... | collective-permute-start | bytes 98312 | tf_op jit(solution)/shard_map/ppermute | solution.py:19
  40.1 6.7 %collective-permute-start.3 = (f32[8192]{0:T(1024)S(1)}, f32[8192]{0:T(1024)S(1)}, u32[]{:S(2)}, u32[]{:S(2)}) collective-permute-start(f32[8192]{0:T(1024)S(1)} %get-tuple-element.7), channel_id=1, source_target_pairs={{1,0},{2,1},{3,2},{4,3},{5,4},{6,5},{7,6},{9,8},{10,9},{11,10},{12... | collective-permute-start | bytes 98312 | tf_op jit(solution)/shard_map/ppermute | solution.py:19
  48.6 10.0 %collective-permute-start.7 = (f32[1,8192]{1,0:T(1,128)S(1)}, f32[1,8192]{1,0:T(1,128)S(1)}, u32[]{:S(2)}, u32[]{:S(2)}) collective-permute-start(f32[1,8192]{1,0:T(1,128)S(1)} %get-tuple-element.36), channel_id=1, source_target_pairs={{0,8},{8,16},{16,24},{24,32},{32,40},{40,48},{48,56},{56,64},{64,7... | collective-permute-start | bytes 98312 | tf_op jit(solution)/shard_map/ppermute | solution.py:29
  50.6 9.4 %collective-permute-start.8 = (f32[1,8192]{1,0:T(1,128)S(1)}, f32[1,8192]{1,0:T(1,128)S(1)}, u32[]{:S(2)}, u32[]{:S(2)}) collective-permute-start(f32[1,8192]{1,0:T(1,128)S(1)} %get-tuple-element.37), channel_id=1, source_target_pairs={{8,0},{16,8},{24,16},{32,24},{40,32},{48,40},{56,48},{64,56},{72,6... | collective-permute-start | bytes 98312 | tf_op jit(solution)/shard_map/ppermute | solution.py:30
  60.8 10.0 %collective-permute-start.9 = (f32[1,8192]{1,0:T(1,128)S(1)}, f32[1,8192]{1,0:T(1,128)S(1)}, u32[]{:S(2)}, u32[]{:S(2)}) collective-permute-start(f32[1,8192]{1,0:T(1,128)S(1)} %get-tuple-element.32), channel_id=1, source_target_pairs={{0,8},{8,16},{16,24},{24,32},{32,40},{40,48},{48,56},{56,64},{64,7... | collective-permute-start | bytes 98312 | tf_op jit(solution)/shard_map/ppermute | solution.py:29
  62.8 9.5 %collective-permute-start.10 = (f32[1,8192]{1,0:T(1,128)S(1)}, f32[1,8192]{1,0:T(1,128)S(1)}, u32[]{:S(2)}, u32[]{:S(2)}) collective-permute-start(f32[1,8192]{1,0:T(1,128)S(1)} %get-tuple-element.33), channel_id=1, source_target_pairs={{8,0},{16,8},{24,16},{32,24},{40,32},{48,40},{56,48},{64,56},{72,6... | collective-permute-start | bytes 98312 | tf_op jit(solution)/shard_map/ppermute | solution.py:30
  73.1 16.8 %collective-permute-start.11 = (f32[8192]{0:T(1024)S(1)}, f32[8192]{0:T(1024)S(1)}, u32[]{:S(2)}, u32[]{:S(2)}) collective-permute-start(f32[8192]{0:T(1024)S(1)} %get-tuple-element.5), channel_id=1, source_target_pairs={{1,0},{2,1},{3,2},{4,3},{5,4},{6,5},{7,6},{9,8},{10,9},{11,10},{12... | collective-permute-start | bytes 98312 | tf_op jit(solution)/shard_map/ppermute | solution.py:19
  75.5 14.4 %collective-permute-start.12 = (f32[8192]{0:T(1024)S(1)}, f32[8192]{0:T(1024)S(1)}, u32[]{:S(2)}, u32[]{:S(2)}) collective-permute-start(f32[8192]{0:T(1024)S(1)} %get-tuple-element.6), channel_id=1, source_target_pairs={{0,1},{1,2},{2,3},{3,4},{4,5},{5,6},{6,7},{8,9},{9,10},{10,11},{11... | collective-permute-start | bytes 98312 | tf_op jit(solution)/shard_map/ppermute | solution.py:19
  80.2 9.9 %collective-permute-start.13 = (f32[1,8192]{1,0:T(1,128)S(1)}, f32[1,8192]{1,0:T(1,128)S(1)}, u32[]{:S(2)}, u32[]{:S(2)}) collective-permute-start(f32[1,8192]{1,0:T(1,128)S(1)} %get-tuple-element.28), channel_id=1, source_target_pairs={{0,8},{8,16},{16,24},{24,32},{32,40},{40,48},{48,56},{56,64},{64,7... | collective-permute-start | bytes 98312 | tf_op jit(solution)/shard_map/ppermute | solution.py:29
  82.1 9.4 %collective-permute-start.14 = (f32[1,8192]{1,0:T(1,128)S(1)}, f32[1,8192]{1,0:T(1,128)S(1)}, u32[]{:S(2)}, u32[]{:S(2)}) collective-permute-start(f32[1,8192]{1,0:T(1,128)S(1)} %get-tuple-element.29), channel_id=1, source_target_pairs={{8,0},{16,8},{24,16},{32,24},{40,32},{48,40},{56,48},{64,56},{72,6... | collective-permute-start | bytes 98312 | tf_op jit(solution)/shard_map/ppermute | solution.py:30
  92.3 10.0 %collective-permute-start.15 = (f32[1,8192]{1,0:T(1,128)S(1)}, f32[1,8192]{1,0:T(1,128)S(1)}, u32[]{:S(2)}, u32[]{:S(2)}) collective-permute-start(f32[1,8192]{1,0:T(1,128)S(1)} %get-tuple-element.24), channel_id=1, source_target_pairs={{0,8},{8,16},{16,24},{24,32},{32,40},{40,48},{48,56},{56,64},{64,7... | collective-permute-start | bytes 98312 | tf_op jit(solution)/shard_map/ppermute | solution.py:29
  94.2 9.5 %collective-permute-start.16 = (f32[1,8192]{1,0:T(1,128)S(1)}, f32[1,8192]{1,0:T(1,128)S(1)}, u32[]{:S(2)}, u32[]{:S(2)}) collective-permute-start(f32[1,8192]{1,0:T(1,128)S(1)} %get-tuple-element.25), channel_id=1, source_target_pairs={{8,0},{16,8},{24,16},{32,24},{40,32},{48,40},{56,48},{64,56},{72,6... | collective-permute-start | bytes 98312 | tf_op jit(solution)/shard_map/ppermute | solution.py:30
  104.5 10.0 %collective-permute-start.17 = (f32[1,8192]{1,0:T(1,128)S(1)}, f32[1,8192]{1,0:T(1,128)S(1)}, u32[]{:S(2)}, u32[]{:S(2)}) collective-permute-start(f32[1,8192]{1,0:T(1,128)S(1)} %get-tuple-element.22), channel_id=1, source_target_pairs={{0,8},{8,16},{16,24},{24,32},{32,40},{40,48},{48,56},{56,64},{64,7... | collective-permute-start | bytes 98312 | tf_op jit(solution)/shard_map/ppermute | solution.py:29
  106.5 9.5 %collective-permute-start.18 = (f32[1,8192]{1,0:T(1,128)S(1)}, f32[1,8192]{1,0:T(1,128)S(1)}, u32[]{:S(2)}, u32[]{:S(2)}) collective-permute-start(f32[1,8192]{1,0:T(1,128)S(1)} %get-tuple-element.23), channel_id=1, source_target_pairs={{8,0},{16,8},{24,16},{32,24},{40,32},{48,40},{56,48},{64,56},{72,6... | collective-permute-start | bytes 98312 | tf_op jit(solution)/shard_map/ppermute | solution.py:30
where the time goes:
time: 118 us; the launch traced here: 117 us
  starting transfers between devices  81.5 us (69%)
  other arithmetic  22.4 us (19%)
  waiting for transfers between devices  9.9 us (8%)
  local copies, waits for them, and re-layouts  3.3 us (3%)
    ppermute x6, starting transfers between devices, padded_2(): after = lax.ppermute(leading, axis, down)  48.1 us
    ppermute x7, starting transfers between devices, passed_along(): return lax.ppermute(block, axis, route)  21.8 us
    add x1, other arithmetic, lookup(): result + jnp.where(class_codes == code, class_table[code], jnp.float32(0.0))  12.7 us
    ppermute x6, starting transfers between devices, padded_2(): before = lax.ppermute(last, axis, up)  11.5 us
    ppermute x6, waiting for transfers between devices, padded_2(): after = lax.ppermute(leading, axis, down)  6.98 us
    add x4, other arithmetic, relax_sweep(): return (centre_cells + update, update)  4.03 us
    ppermute x7, waiting for transfers between devices, passed_along(): return lax.ppermute(block, axis, route)  2.91 us
  transfers between devices with their start and end apart: 19, of which 6 were waited for; matrix products, arithmetic and copies ran while one was open for 16% of the time, Pallas kernels for 0%

commit v1 on v0

v1 whole, which is shorter than its diff:
```python
import functools

import jax
import jax.numpy as jnp
from jax import lax
from jax.experimental import pallas as pl
from jax.experimental.pallas import tpu as pltpu
from jax.sharding import PartitionSpec as P

CLASSES = 16
OUTER = 2
SWEEPS = 3
VIA_UNIT = 2.0
LOWER_BOUND = 0.05
UPPER_BOUND = 2.0
LANES = 128
SUB = 8
MESH = pl.DeviceIdType.MESH


def chebyshev_terms(count):
    centre_value = 0.5 * (UPPER_BOUND + LOWER_BOUND)
    half_width = 0.5 * (UPPER_BOUND - LOWER_BOUND)
    sigma = centre_value / half_width
    rho_last = 1.0 / sigma
    terms = [(0.0, 1.0 / centre_value)]
    for index in range(1, count):
        rho_next = 1.0 / (2.0 * sigma - rho_last)
        terms.append((rho_next * rho_last, 2.0 * rho_next / half_width))
        rho_last = rho_next
    return terms


def kernel(
    rows,
    blocks,
    table,
    class_hbm,
    loads_hbm,
    volts_hbm,
    cells_hbm,
    counts_hbm,
    out_hbm,
    x,
    cls,
    to_right,
    to_left,
    to_up,
    to_down,
    drawn,
    right_side,
    links_in,
    halo,
    own_cells,
    own_counts,
    low_cells,
    low_counts,
    picked,
    below,
    above,
    scale,
    flow,
    in_sem,
    class_sem,
    via_sem,
    out_sem,
    send_sem,
    recv_sem,
):
    tile = lax.axis_index("tile")
    layer = lax.axis_index("layer")
    tiles = lax.axis_size("tile")
    layers = lax.axis_size("layer")
    next_tile = {"tile": lax.rem(tile + 1, tiles)}
    prev_tile = {"tile": lax.rem(tile + tiles - 1, tiles)}
    next_layer = {"layer": lax.rem(layer + 1, layers)}
    prev_layer = {"layer": lax.rem(layer + layers - 1, layers)}
    last = rows - 1
    sweeps = OUTER * SWEEPS

    cells_in = pltpu.make_async_copy(cells_hbm, own_cells, via_sem.at[0])
    counts_in = pltpu.make_async_copy(counts_hbm, own_counts, via_sem.at[1])
    cells_in.start()

    def load_volts(r, _):
        pltpu.make_async_copy(
            volts_hbm.at[r // SUB, :, lax.rem(r, SUB)], x.at[0, r], in_sem.at[0]
        ).start()
        return 0

    def load_links(r, _):
        for k in range(2):
            pltpu.make_async_copy(
                class_hbm.at[k, r // SUB, :, lax.rem(r, SUB)], cls.at[k, r], class_sem.at[0]
            ).start()
        return 0

    def load_loads(r, _):
        pltpu.make_async_copy(
            loads_hbm.at[r // SUB, :, lax.rem(r, SUB)], drawn.at[r], in_sem.at[1]
        ).start()
        return 0

    lax.fori_loop(0, rows, load_volts, 0)
    counts_in.start()
    lax.fori_loop(0, rows, load_links, 0)
    lax.fori_loop(0, rows, load_loads, 0)

    barrier = pltpu.get_barrier_semaphore()
    for peer in (next_tile, prev_tile, next_layer, prev_layer):
        pl.semaphore_signal(barrier, inc=1, device_id=peer, device_id_type=MESH)

    sent = []

    def remote(src, dst, peer):
        slot = len(sent)
        copy = pltpu.make_async_remote_copy(
            src_ref=src,
            dst_ref=dst,
            send_sem=send_sem.at[slot],
            recv_sem=recv_sem.at[slot],
            device_id=peer,
            device_id_type=MESH,
        )
        copy.start()
        sent.append(copy)
        return copy

    def exchange(step):
        upper = remote(x.at[step, last], halo.at[step, 0], next_tile)
        lower = remote(x.at[step, 0], halo.at[step, 1], prev_tile)
        return upper, lower

    lane = lax.broadcasted_iota(jnp.int32, (blocks, LANES), 1)
    zero = jnp.float32(0.0)

    def pick(step, cells):
        def body(r, acc):
            return jnp.where(cells == r, x[step, r], acc)

        return lax.fori_loop(0, rows, body, jnp.zeros((blocks, LANES), jnp.float32), unroll=True)

    cells_in.wait()
    counts_in.wait()
    pl.semaphore_wait(barrier, 4)
    cells_up = remote(own_cells, low_cells, next_layer)
    pltpu.make_async_copy(x.at[1], x.at[0], in_sem.at[0]).wait()
    picked[0] = pick(0, own_cells[...])
    volts_up = remote(picked.at[0], below.at[0], next_layer)
    halos = exchange(0)
    counts_up = remote(own_counts, low_counts, next_layer)

    pltpu.make_async_copy(cls, cls, class_sem.at[0]).wait()
    table_lane = lax.broadcasted_iota(jnp.int32, (SUB, LANES), 1)
    values = jnp.zeros((SUB, LANES), jnp.float32)
    for code in range(CLASSES):
        values = jnp.where(table_lane == code, table[0, code], values)

    def look_up(codes):
        return jnp.concatenate(
            [
                jnp.take_along_axis(
                    values, codes[SUB * k : SUB * (k + 1)], axis=1, mode="promise_in_bounds"
                )
                for k in range(blocks // SUB)
            ],
            axis=0,
        )

    to_down[last] = jnp.where(tile == tiles - 1, zero, look_up(cls[1, last]))
    links_down = remote(to_down.at[last], links_in, next_tile)

    block_ids = lax.broadcasted_iota(jnp.int32, (blocks, LANES), 0)
    at_end = jnp.logical_and(block_ids == blocks - 1, lane == LANES - 1)

    def look_up_row(r, _):
        to_right[r] = jnp.where(at_end, zero, look_up(cls[0, r]))

        @pl.when(r < last)
        def _():
            to_down[r] = look_up(cls[1, r])

        return 0

    lax.fori_loop(0, rows, look_up_row, 0)

    cells_up.wait_recv()
    picked[1] = pick(0, low_cells[...])
    volts_down = remote(picked.at[1], above.at[0], prev_layer)

    counts_up.wait_recv()
    links_down.wait_recv()
    pltpu.make_async_copy(drawn, drawn, in_sem.at[1]).wait()

    def right_of(v):
        turned = pltpu.roll(v, LANES - 1, 1)
        return jnp.where(lane == LANES - 1, pltpu.roll(turned, blocks - 1, 0), turned)

    def left_of(v):
        turned = pltpu.roll(v, 1, 1)
        return jnp.where(lane == 0, pltpu.roll(turned, 1, 0), turned)

    scale[0] = VIA_UNIT * own_counts[...].astype(jnp.float32)
    scale[1] = jnp.where(layer == 0, zero, VIA_UNIT * low_counts[...].astype(jnp.float32))
    scale[2] = jnp.zeros((blocks, LANES), jnp.float32)
    scale[3] = jnp.zeros((blocks, LANES), jnp.float32)
    sent_links = []

    def coefficients(r, up, down):
        own = own_cells[...] == r
        low = low_cells[...] == r
        across = to_right[r]
        before = left_of(across)
        diagonal = (
            across + before + up + down + jnp.where(own, scale[0], zero) + jnp.where(low, scale[1], zero)
        )
        inverse = 1.0 / diagonal
        to_right[r] = inverse * across
        to_left[r] = inverse * before
        to_up[r] = inverse * up
        drawn[r] = inverse * drawn[r]
        scale[2] = jnp.where(own, inverse, scale[2])
        scale[3] = jnp.where(low, inverse, scale[3])
        return inverse * down

    def coefficients_row(r, _):
        flow[r] = coefficients(r, to_down[r - 1], to_down[r])
        return 0

    flow[0] = coefficients(0, links_in[...], to_down[0])
    lax.fori_loop(1, rows, coefficients_row, 0)
    scale[2] = scale[2] * scale[0]
    scale[3] = scale[3] * scale[1]

    def sweep_row(step, r, upper, lower, first_of_step):
        here = x[step, r]
        if first_of_step:
            side = (
                jnp.where(own_cells[...] == r, scale[0], zero)
                + jnp.where(low_cells[...] == r, scale[1], zero)
                - drawn[r]
            )
            right_side[r] = side
        else:
            side = right_side[r]
        fore, aft = factors[step % SWEEPS]
        total = (
            side
            + to_right[r] * right_of(here)
            + to_left[r] * left_of(here)
            + to_up[r] * upper
            + flow[r] * lower
        )
        update = jnp.float32(aft) * (total - here)
        if step % SWEEPS:
            update = update + jnp.float32(fore) * (here - x[step - 1, r])
        x[step + 1, r] = here + update

    factors = chebyshev_terms(SWEEPS)
    waits = None
    out_copies = []
    for step in range(sweeps):
        first = step % SWEEPS == 0
        if first:
            volts_up.wait_recv()
            volts_down.wait_recv()
            outer = step // SWEEPS
            top = jnp.where(layer == layers - 1, jnp.float32(1.0), above[outer])
            scale[0] = scale[2] * top
            scale[1] = scale[3] * below[outer]

        def inner_row(r, _, step=step, first=first):
            sweep_row(step, r, x[step, r - 1], x[step, r + 1], first)
            if step == sweeps - 1:
                pltpu.make_async_copy(
                    x.at[sweeps, r], out_hbm.at[r // SUB, :, lax.rem(r, SUB)], out_sem
                ).start()
            return 0

        lax.fori_loop(1, last, inner_row, 0)
        halos[0].wait_recv()
        sweep_row(step, 0, halo[step, 0], x[step, 1], first)
        halos[1].wait_recv()
        sweep_row(step, last, x[step, last - 1], halo[step, 1], first)
        if step < sweeps - 1:
            halos = exchange(step + 1)
        if step + 1 < sweeps and (step + 1) % SWEEPS == 0:
            outer = (step + 1) // SWEEPS
            picked[2 * outer] = pick(step + 1, own_cells[...])
            volts_up = remote(picked.at[2 * outer], below.at[outer], next_layer)
            picked[2 * outer + 1] = pick(step + 1, low_cells[...])
            volts_down = remote(picked.at[2 * outer + 1], above.at[outer], prev_layer)
    for r in (0, last):
        pltpu.make_async_copy(x.at[sweeps, r], out_hbm.at[r // SUB, :, r % SUB], out_sem).start()
    pltpu.make_async_copy(x.at[sweeps], x.at[sweeps], out_sem).wait()
    for copy in sent:
        copy.wait_send()


def local(class_index, class_conductance, loads, start_volts, via_cells, via_counts):
    rows, cols = loads.shape[1:]
    blocks = cols // LANES
    groups = rows // SUB

    def folded(a):
        lead = a.shape[:-2]
        a = a.reshape(*lead, groups, SUB, blocks, LANES)
        return jnp.swapaxes(a, -3, -2)

    classes = folded(class_index[0])
    drawn = folded(loads[0])
    volts = folded(start_volts[0])
    cells = via_cells.reshape(blocks, LANES)
    counts = via_counts.reshape(blocks, LANES)
    grid = (rows, blocks, LANES)
    row = (blocks, LANES)
    f32, i32 = jnp.float32, jnp.int32
    copies = 2 * OUTER * SWEEPS + 1 + 2 + 2 * OUTER
    vmem = pltpu.VMEM


    out = pl.pallas_call(
        functools.partial(kernel, rows, blocks),
        out_shape=jax.ShapeDtypeStruct((groups, blocks, SUB, LANES), f32),
        in_specs=[pl.BlockSpec(memory_space=pltpu.SMEM)] + [pl.BlockSpec(memory_space=pl.ANY)] * 5,
        out_specs=pl.BlockSpec(memory_space=pl.ANY),
        scratch_shapes=[
            vmem((OUTER * SWEEPS + 1, *grid), f32),
            vmem((2, *grid), i32),
            vmem(grid, f32),
            vmem(grid, f32),
            vmem(grid, f32),
            vmem(grid, f32),
            vmem(grid, f32),
            vmem(grid, f32),
            vmem(row, f32),
            vmem((OUTER * SWEEPS, 2, *row), f32),
            vmem(row, i32),
            vmem(row, i32),
            vmem(row, i32),
            vmem(row, i32),
            vmem((2 * OUTER, *row), f32),
            vmem((OUTER, *row), f32),
            vmem((OUTER, *row), f32),
            vmem((4, *row), f32),
            vmem(grid, f32),
            pltpu.SemaphoreType.DMA((2,)),
            pltpu.SemaphoreType.DMA((1,)),
            pltpu.SemaphoreType.DMA((2,)),
            pltpu.SemaphoreType.DMA,
            pltpu.SemaphoreType.DMA((copies,)),
            pltpu.SemaphoreType.DMA((copies,)),
        ],
        compiler_params=pltpu.CompilerParams(
            collective_id=0, has_side_effects=True, vmem_limit_bytes=60 * 1024 * 1024
        ),
    )(class_conductance, classes, drawn, volts, cells, counts)
    return jnp.swapaxes(out, 1, 2).reshape(1, rows, cols)


def solution(mesh):
    placed = (
        P("layer", None, "tile", None),
        P("layer", None),
        P("layer", "tile", None),
        P("layer", "tile", None),
        P("layer", "tile"),
        P("layer", "tile"),
    )
    return jax.shard_map(
        local, mesh=mesh, in_specs=placed, out_specs=P("layer", "tile", None), check_vma=False
    )
```

time: 118 us -> 51.2 us (0.43)
  the two profiles are of different devices: /device:TPU:96 before, /device:TPU:6 now
where the time goes in v1:
time: 51.2 us; the launch traced here: 50.9 us
  Pallas kernels  49.1 us (96%)
  local copies, waits for them, and re-layouts  1.87 us (4%)
    pallas_call x1, Pallas kernels, local(): pl.pallas_call(functools.partial(kernel, rows, blocks), out_shape=jax.Sha...  49.1 us
    unnamed x1, local copies, waits for them, and re-layouts  1.87 us

profile of v1, /device:TPU:6, one launch (start us, length us, event | category | flops | bytes accessed | tf_op | source)
XLA Modules:
  0.0 50.9 jit_solution(2265415709807890711)
XLA Ops:
  0.0 49.1 %shard_map.64 = f32[2,64,8,128]{3,2,1,0:T(8,128)} custom-call(f32[1,16]{1,0:T(1,128)} %table.1, s32[2,2,64,8,128]{4,3,2,1,0:T(8,128)} %bitcast.15, f32[2,64,8,128]{3,2,1,0:T(8,128)} %bitcast.16, f32[2,64,8,128]{3,2,1,0:T(8,128)} %bitcast.17, s32[64,128]{1,0:T(8,128)} %bitcast.18, s32[64,128]{1,0:T(8,128)} %bitcast.19), custom_call_target="tpu_custom_call" | custom-call | tf_op jit(solution)/shard_map/pallas_call | solution.py:322
  49.1 1.9 %copy.8 = f32[1,16,8192]{2,1,0:T(8,128)} copy(f32[1,16,8192]{2,1,0:T(8,128)} %bitcast.14) | data formatting | bytes 1048576

commit v2 on v1

v2 whole, which is shorter than its diff:
```python
import functools

import jax
import jax.numpy as jnp
from jax import lax
from jax.experimental import pallas as pl
from jax.experimental.pallas import tpu as pltpu
from jax.sharding import PartitionSpec as P

CLASSES = 16
OUTER = 2
SWEEPS = 3
VIA_UNIT = 2.0
LOWER_BOUND = 0.05
UPPER_BOUND = 2.0
LANES = 128
SUB = 8
MESH = pl.DeviceIdType.MESH


def chebyshev_terms(count):
    centre_value = 0.5 * (UPPER_BOUND + LOWER_BOUND)
    half_width = 0.5 * (UPPER_BOUND - LOWER_BOUND)
    sigma = centre_value / half_width
    rho_last = 1.0 / sigma
    terms = [(0.0, 1.0 / centre_value)]
    for index in range(1, count):
        rho_next = 1.0 / (2.0 * sigma - rho_last)
        terms.append((rho_next * rho_last, 2.0 * rho_next / half_width))
        rho_last = rho_next
    return terms


def kernel(
    rows,
    blocks,
    table,
    class_hbm,
    loads_hbm,
    volts_hbm,
    cells_hbm,
    counts_hbm,
    out_hbm,
    x,
    cls,
    links,
    drawn,
    right_side,
    down_links,
    links_in,
    ghost_links,
    halo,
    halo_pair,
    halo_side,
    ghost,
    own_cells,
    own_counts,
    low_cells,
    low_counts,
    picked,
    below,
    above,
    scale,
    in_sem,
    class_sem,
    via_sem,
    out_sem,
    send_sem,
    recv_sem,
):
    tile = lax.axis_index("tile")
    layer = lax.axis_index("layer")
    tiles = lax.axis_size("tile")
    layers = lax.axis_size("layer")
    next_tile = {"tile": lax.rem(tile + 1, tiles)}
    prev_tile = {"tile": lax.rem(tile + tiles - 1, tiles)}
    next_layer = {"layer": lax.rem(layer + 1, layers)}
    prev_layer = {"layer": lax.rem(layer + layers - 1, layers)}
    last = rows - 1
    sweeps = OUTER * SWEEPS
    factors = chebyshev_terms(SWEEPS)
    f32 = jnp.float32
    zero = f32(0.0)
    row_shape = (blocks, LANES)

    cells_in = pltpu.make_async_copy(cells_hbm, own_cells, via_sem.at[0])
    counts_in = pltpu.make_async_copy(counts_hbm, own_counts, via_sem.at[1])
    cells_in.start()

    def load_volts(r, _):
        pltpu.make_async_copy(
            volts_hbm.at[r // SUB, :, lax.rem(r, SUB)], x.at[0, r], in_sem.at[0]
        ).start()
        return 0

    def load_links(r, _):
        for k in range(2):
            pltpu.make_async_copy(
                class_hbm.at[k, r // SUB, :, lax.rem(r, SUB)], cls.at[k, r], class_sem.at[0]
            ).start()
        return 0

    def load_loads(r, _):
        pltpu.make_async_copy(
            loads_hbm.at[r // SUB, :, lax.rem(r, SUB)], drawn.at[r], in_sem.at[1]
        ).start()
        return 0

    barrier = pltpu.get_barrier_semaphore()
    for peer in (next_layer, prev_layer, next_tile, prev_tile):
        pl.semaphore_signal(barrier, inc=1, device_id=peer, device_id_type=MESH)

    lax.fori_loop(0, rows, load_volts, 0)
    counts_in.start()
    lax.fori_loop(0, rows, load_links, 0)
    lax.fori_loop(0, rows, load_loads, 0)

    sent = []

    def remote(src, dst, peer):
        slot = len(sent)
        copy = pltpu.make_async_remote_copy(
            src_ref=src,
            dst_ref=dst,
            send_sem=send_sem.at[slot],
            recv_sem=recv_sem.at[slot],
            device_id=peer,
            device_id_type=MESH,
        )
        copy.start()
        sent.append(copy)
        return copy

    lane = lax.broadcasted_iota(jnp.int32, row_shape, 1)
    block = lax.broadcasted_iota(jnp.int32, row_shape, 0)

    def pick(step, cells, acc, start, stop):
        def body(r, acc):
            return jnp.where(cells == r, x[step, r], acc)

        return lax.fori_loop(start, stop, body, acc, unroll=True)

    table_lane = lax.broadcasted_iota(jnp.int32, (SUB, LANES), 1)
    values = jnp.zeros((SUB, LANES), f32)
    for code in range(CLASSES):
        values = jnp.where(table_lane == code, table[0, code], values)

    def look_up(codes):
        return jnp.concatenate(
            [
                jnp.take_along_axis(
                    values, codes[SUB * k : SUB * (k + 1)], axis=1, mode="promise_in_bounds"
                )
                for k in range(blocks // SUB)
            ],
            axis=0,
        )

    cells_in.wait()
    counts_in.wait()
    pltpu.make_async_copy(x.at[1], x.at[0], in_sem.at[0]).wait()
    picked[0] = pick(0, own_cells[...], jnp.zeros(row_shape, f32), 0, rows)
    pltpu.make_async_copy(cls, cls, class_sem.at[0]).wait()
    down_links[last] = jnp.where(tile == tiles - 1, zero, look_up(cls[1, last]))

    pl.semaphore_wait(barrier, 4)
    cells_up = remote(own_cells, low_cells, next_layer)
    links_down = remote(down_links.at[last], links_in, next_tile)
    counts_up = remote(own_counts, low_counts, next_layer)
    volts_up = remote(picked.at[0], below.at[0], next_layer)

    def send_halo(outer):
        step = outer * SWEEPS
        return (
            remote(x.at[step, last], halo.at[outer, 0], next_tile),
            remote(x.at[step, 0], halo.at[outer, 1], prev_tile),
        )

    halos = send_halo(0)

    at_end = jnp.logical_and(block == blocks - 1, lane == LANES - 1)

    def look_up_row(r, _):
        links[0, r] = jnp.where(at_end, zero, look_up(cls[0, r]))

        @pl.when(r < last)
        def _():
            down_links[r] = look_up(cls[1, r])

        return 0

    lax.fori_loop(0, rows, look_up_row, 0)

    cells_up.wait_recv()
    picked[1] = pick(0, low_cells[...], jnp.zeros(row_shape, f32), 0, rows)
    volts_down = remote(picked.at[1], above.at[0], prev_layer)

    def right_of(v):
        turned = pltpu.roll(v, LANES - 1, 1)
        return jnp.where(lane == LANES - 1, pltpu.roll(turned, blocks - 1, 0), turned)

    def left_of(v):
        turned = pltpu.roll(v, 1, 1)
        return jnp.where(lane == 0, pltpu.roll(turned, 1, 0), turned)

    counts_up.wait_recv()
    pltpu.make_async_copy(drawn, drawn, in_sem.at[1]).wait()
    scale[0] = VIA_UNIT * own_counts[...].astype(f32)
    scale[1] = jnp.where(layer == 0, zero, VIA_UNIT * low_counts[...].astype(f32))
    scale[2] = jnp.zeros(row_shape, f32)
    scale[3] = jnp.zeros(row_shape, f32)

    def coefficients(r, up, down):
        own = own_cells[...] == r
        low = low_cells[...] == r
        right = links[0, r]
        left = left_of(right)
        diagonal = right + left + up + down
        diagonal = diagonal + jnp.where(own, scale[0], zero) + jnp.where(low, scale[1], zero)
        inverse = 1.0 / diagonal
        links[0, r] = inverse * right
        links[1, r] = inverse * left
        links[2, r] = inverse * up
        links[3, r] = inverse * down
        drawn[r] = inverse * drawn[r]
        scale[2] = jnp.where(own, inverse, scale[2])
        scale[3] = jnp.where(low, inverse, scale[3])

    def coefficients_row(r, _):
        coefficients(r, down_links[r - 1], down_links[r])
        return 0

    lax.fori_loop(1, rows, coefficients_row, 0)
    links_down.wait_recv()
    coefficients(0, links_in[...], down_links[0])
    scale[2] = scale[2] * scale[0]
    scale[3] = scale[3] * scale[1]
    ghosts_ready = (
        remote(links.at[:, last], ghost_links.at[0], next_tile),
        remote(links.at[:, 0], ghost_links.at[1], prev_tile),
    )

    def base_row(step, r, upper, lower):
        here = x[step, r]
        total = links[0, r] * right_of(here) + links[1, r] * left_of(here) - drawn[r]
        if upper is not None:
            total = total + links[2, r] * upper
        if lower is not None:
            total = total + links[3, r] * lower
        x[step + 1, r] = here + f32(factors[0][1]) * (total - here)

    def finish_row(step, r, flow):
        side = jnp.where(own_cells[...] == r, scale[0], zero) + jnp.where(
            low_cells[...] == r, scale[1], zero
        )
        right_side[step // SWEEPS, r] = side - drawn[r]
        if flow is not None:
            side = side + flow
        x[step + 1, r] = x[step + 1, r] + f32(factors[0][1]) * side

    def advanced(step, here, before, side, weights, upper, lower):
        fore, aft = factors[step % SWEEPS]
        total = (
            side
            + weights[0] * right_of(here)
            + weights[1] * left_of(here)
            + weights[2] * upper
            + weights[3] * lower
        )
        return here + f32(aft) * (total - here) + f32(fore) * (here - before)

    def sweep_row(step, r, upper, lower):
        weights = [links[k, r] for k in range(4)]
        x[step + 1, r] = advanced(
            step, x[step, r], x[step - 1, r], right_side[step // SWEEPS, r], weights, upper, lower
        )

    def send_out(r):
        pltpu.make_async_copy(
            x.at[sweeps, r], out_hbm.at[r // SUB, :, lax.rem(r, SUB)], out_sem
        ).start()

    for outer in range(OUTER):
        step = outer * SWEEPS
        final = outer == OUTER - 1

        def base(r, _, step=step):
            base_row(step, r, x[step, r - 1], x[step, r + 1])
            return 0

        base_row(step, 0, None, x[step, 1])
        base_row(step, last, x[step, last - 1], None)
        lax.fori_loop(1, last, base, 0)

        volts_up.wait_recv()
        volts_down.wait_recv()
        scale[0] = scale[2] * jnp.where(layer == layers - 1, f32(1.0), above[outer])
        scale[1] = scale[3] * below[outer]
        finish_row(step, 1, None)
        finish_row(step, last - 1, None)
        halos[0].wait_recv()
        finish_row(step, 0, links[2, 0] * halo[outer, 0])
        halos[1].wait_recv()
        finish_row(step, last, links[3, last] * halo[outer, 1])
        pairs = (
            remote(x.at[step + 1, pl.ds(last - 1, 2)], halo_pair.at[outer, 0], next_tile),
            remote(x.at[step + 1, pl.ds(0, 2)], halo_pair.at[outer, 1], prev_tile),
            remote(right_side.at[outer, last], halo_side.at[outer, 0], next_tile),
            remote(right_side.at[outer, 0], halo_side.at[outer, 1], prev_tile),
        )

        def finish(r, _, step=step):
            finish_row(step, r, None)
            return 0

        def second(r, _, step=step):
            sweep_row(step + 1, r, x[step + 1, r - 1], x[step + 1, r + 1])
            return 0

        def third(r, _, step=step, final=final):
            sweep_row(step + 2, r, x[step + 2, r - 1], x[step + 2, r + 1])
            if final:
                send_out(r)
            return 0

        lax.fori_loop(2, last - 1, finish, 0)
        lax.fori_loop(1, last, second, 0)
        lax.fori_loop(2, last - 1, third, 0)
        if not final:
            for k, cells in enumerate((own_cells, low_cells)):
                picked[2 * outer + 2 + k] = pick(
                    step + 3, cells[...], jnp.zeros(row_shape, f32), 2, last - 1
                )

        for copy in pairs:
            copy.wait_recv()
        if outer == 0:
            for copy in ghosts_ready:
                copy.wait_recv()
        one, two, three = step + 1, step + 2, step + 3
        upper = halo_pair[outer, 0, 1]
        lower = halo_pair[outer, 1, 0]
        ghost[0] = advanced(
            one, upper, halo[outer, 0], halo_side[outer, 0], ghost_links[0], halo_pair[outer, 0, 0], x[one, 0]
        )
        ghost[1] = advanced(
            one, lower, halo[outer, 1], halo_side[outer, 1], ghost_links[1], x[one, last], halo_pair[outer, 1, 1]
        )
        sweep_row(one, 0, upper, x[one, 1])
        sweep_row(one, last, x[one, last - 1], lower)
        sweep_row(two, 0, ghost[0], x[two, 1])
        sweep_row(two, last, x[two, last - 1], ghost[1])
        if final:
            send_out(0)
            send_out(last)
        else:
            halos = send_halo(outer + 1)
        sweep_row(two, 1, x[two, 0], x[two, 2])
        sweep_row(two, last - 1, x[two, last - 2], x[two, last])
        if final:
            send_out(1)
            send_out(last - 1)
        else:
            for k, cells in enumerate((own_cells, low_cells)):
                slot = 2 * outer + 2 + k
                acc = pick(three, cells[...], picked[slot], 0, 2)
                picked[slot] = pick(three, cells[...], acc, last - 1, rows)
                if k == 0:
                    volts_up = remote(picked.at[slot], below.at[outer + 1], next_layer)
                else:
                    volts_down = remote(picked.at[slot], above.at[outer + 1], prev_layer)

    pltpu.make_async_copy(x.at[sweeps], x.at[sweeps], out_sem).wait()
    for copy in sent:
        copy.wait_send()


def local(class_index, class_conductance, loads, start_volts, via_cells, via_counts):
    rows, cols = loads.shape[1:]
    blocks = cols // LANES
    groups = rows // SUB

    def folded(a):
        lead = a.shape[:-2]
        a = a.reshape(*lead, groups, SUB, blocks, LANES)
        return jnp.swapaxes(a, -3, -2)

    classes = folded(class_index[0])
    drawn = folded(loads[0])
    volts = folded(start_volts[0])
    cells = via_cells.reshape(blocks, LANES)
    counts = via_counts.reshape(blocks, LANES)
    grid = (rows, blocks, LANES)
    row = (blocks, LANES)
    f32, i32 = jnp.float32, jnp.int32
    copies = 5 + 2 * (OUTER - 1) + 2 * OUTER + 4 * OUTER + 2
    vmem = pltpu.VMEM


    out = pl.pallas_call(
        functools.partial(kernel, rows, blocks),
        out_shape=jax.ShapeDtypeStruct((groups, blocks, SUB, LANES), f32),
        in_specs=[pl.BlockSpec(memory_space=pltpu.SMEM)] + [pl.BlockSpec(memory_space=pl.ANY)] * 5,
        out_specs=pl.BlockSpec(memory_space=pl.ANY),
        scratch_shapes=[
            vmem((OUTER * SWEEPS + 1, *grid), f32),
            vmem((2, *grid), i32),
            vmem((4, *grid), f32),
            vmem(grid, f32),
            vmem((OUTER, *grid), f32),
            vmem(grid, f32),
            vmem(row, f32),
            vmem((2, 4, *row), f32),
            vmem((OUTER, 2, *row), f32),
            vmem((OUTER, 2, 2, *row), f32),
            vmem((OUTER, 2, *row), f32),
            vmem((2, *row), f32),
            vmem(row, i32),
            vmem(row, i32),
            vmem(row, i32),
            vmem(row, i32),
            vmem((2 * OUTER, *row), f32),
            vmem((OUTER, *row), f32),
            vmem((OUTER, *row), f32),
            vmem((4, *row), f32),
            pltpu.SemaphoreType.DMA((2,)),
            pltpu.SemaphoreType.DMA((1,)),
            pltpu.SemaphoreType.DMA((2,)),
            pltpu.SemaphoreType.DMA,
            pltpu.SemaphoreType.DMA((copies,)),
            pltpu.SemaphoreType.DMA((copies,)),
        ],
        compiler_params=pltpu.CompilerParams(
            collective_id=0, has_side_effects=True, vmem_limit_bytes=60 * 1024 * 1024
        ),
    )(class_conductance, classes, drawn, volts, cells, counts)
    return jnp.swapaxes(out, 1, 2).reshape(1, rows, cols)


def solution(mesh):
    placed = (
        P("layer", None, "tile", None),
        P("layer", None),
        P("layer", "tile", None),
        P("layer", "tile", None),
        P("layer", "tile"),
        P("layer", "tile"),
    )
    return jax.shard_map(
        local, mesh=mesh, in_specs=placed, out_specs=P("layer", "tile", None), check_vma=False
    )
```

time: 51.2 us -> 39.5 us (0.77)
  the two profiles are of different devices: /device:TPU:6 before, /device:TPU:4 now
where the time goes in v2:
time: 39.5 us; the launch traced here: 39.2 us
  Pallas kernels  37.4 us (95%)
  local copies, waits for them, and re-layouts  1.87 us (5%)
    pallas_call x1, Pallas kernels, local(): pl.pallas_call(functools.partial(kernel, rows, blocks), out_shape=jax.Sha...  37.4 us
    unnamed x1, local copies, waits for them, and re-layouts  1.87 us

profile of v2, /device:TPU:4, one launch (start us, length us, event | category | flops | bytes accessed | tf_op | source)
XLA Modules:
  0.0 39.2 jit_solution(4878760180190898459)
XLA Ops:
  0.0 37.4 %shard_map.64 = f32[2,64,8,128]{3,2,1,0:T(8,128)} custom-call(f32[1,16]{1,0:T(1,128)} %table.1, s32[2,2,64,8,128]{4,3,2,1,0:T(8,128)} %bitcast.15, f32[2,64,8,128]{3,2,1,0:T(8,128)} %bitcast.16, f32[2,64,8,128]{3,2,1,0:T(8,128)} %bitcast.17, s32[64,128]{1,0:T(8,128)} %bitcast.18, s32[64,128]{1,0:T(8,128)} %bitcast.19), custom_call_target="tpu_custom_call" | custom-call | tf_op jit(solution)/shard_map/pallas_call | solution.py:400
  37.4 1.9 %copy.8 = f32[1,16,8192]{2,1,0:T(8,128)} copy(f32[1,16,8192]{2,1,0:T(8,128)} %bitcast.14) | data formatting | bytes 1048576

commit v3 on v2

--- a/solution.py
+++ b/solution.py
@@ -50,9 +50,9 @@
     links_in,
     ghost_links,
     halo,
-    halo_pair,
-    halo_side,
-    ghost,
+    halo_next,
+    halo_part,
+    part,
     own_cells,
     own_counts,
     low_cells,
@@ -236,8 +236,8 @@
     scale[2] = scale[2] * scale[0]
     scale[3] = scale[3] * scale[1]
     ghosts_ready = (
-        remote(links.at[:, last], ghost_links.at[0], next_tile),
-        remote(links.at[:, 0], ghost_links.at[1], prev_tile),
+        remote(links.at[3, last], ghost_links.at[0], next_tile),
+        remote(links.at[2, 0], ghost_links.at[1], prev_tile),
     )
 
     def base_row(step, r, upper, lower):
@@ -258,22 +258,22 @@
             side = side + flow
         x[step + 1, r] = x[step + 1, r] + f32(factors[0][1]) * side
 
-    def advanced(step, here, before, side, weights, upper, lower):
+    def swept(step, r, upper, lower):
         fore, aft = factors[step % SWEEPS]
+        here = x[step, r]
         total = (
-            side
-            + weights[0] * right_of(here)
-            + weights[1] * left_of(here)
-            + weights[2] * upper
-            + weights[3] * lower
+            right_side[step // SWEEPS, r]
+            + links[0, r] * right_of(here)
+            + links[1, r] * left_of(here)
         )
-        return here + f32(aft) * (total - here) + f32(fore) * (here - before)
-
-    def sweep_row(step, r, upper, lower):
-        weights = [links[k, r] for k in range(4)]
-        x[step + 1, r] = advanced(
-            step, x[step, r], x[step - 1, r], right_side[step // SWEEPS, r], weights, upper, lower
-        )
+        if upper is not None:
+            total = total + links[2, r] * upper
+        if lower is not None:
+            total = total + links[3, r] * lower
+        return here + f32(aft) * (total - here) + f32(fore) * (here - x[step - 1, r])
+
+    def add_flow(step, value, link, other):
+        return value + f32(factors[step % SWEEPS][1]) * (link * other)
 
     def send_out(r):
         pltpu.make_async_copy(
@@ -302,23 +302,26 @@
         finish_row(step, 0, links[2, 0] * halo[outer, 0])
         halos[1].wait_recv()
         finish_row(step, last, links[3, last] * halo[outer, 1])
-        pairs = (
-            remote(x.at[step + 1, pl.ds(last - 1, 2)], halo_pair.at[outer, 0], next_tile),
-            remote(x.at[step + 1, pl.ds(0, 2)], halo_pair.at[outer, 1], prev_tile),
-            remote(right_side.at[outer, last], halo_side.at[outer, 0], next_tile),
-            remote(right_side.at[outer, 0], halo_side.at[outer, 1], prev_tile),
-        )
+        one, two, three = step + 1, step + 2, step + 3
+        edges = [
+            remote(x.at[one, last], halo_next.at[outer, 0], next_tile),
+            remote(x.at[one, 0], halo_next.at[outer, 1], prev_tile),
+        ]
+        part[outer, 0] = swept(one, last, x[one, last - 1], None)
+        edges.append(remote(part.at[outer, 0], halo_part.at[outer, 0], next_tile))
+        part[outer, 1] = swept(one, 0, None, x[one, 1])
+        edges.append(remote(part.at[outer, 1], halo_part.at[outer, 1], prev_tile))
 
         def finish(r, _, step=step):
             finish_row(step, r, None)
             return 0
 
         def second(r, _, step=step):
-            sweep_row(step + 1, r, x[step + 1, r - 1], x[step + 1, r + 1])
+            x[step + 2, r] = swept(step + 1, r, x[step + 1, r - 1], x[step + 1, r + 1])
             return 0
 
         def third(r, _, step=step, final=final):
-            sweep_row(step + 2, r, x[step + 2, r - 1], x[step + 2, r + 1])
+            x[step + 3, r] = swept(step + 2, r, x[step + 2, r - 1], x[step + 2, r + 1])
             if final:
                 send_out(r)
             return 0
@@ -326,37 +329,32 @@
         lax.fori_loop(2, last - 1, finish, 0)
         lax.fori_loop(1, last, second, 0)
         lax.fori_loop(2, last - 1, third, 0)
+        x[three, 1] = swept(two, 1, None, x[two, 2])
+        x[three, last - 1] = swept(two, last - 1, x[two, last - 2], None)
         if not final:
             for k, cells in enumerate((own_cells, low_cells)):
                 picked[2 * outer + 2 + k] = pick(
                     step + 3, cells[...], jnp.zeros(row_shape, f32), 2, last - 1
                 )
 
-        for copy in pairs:
+        for copy in edges:
             copy.wait_recv()
         if outer == 0:
             for copy in ghosts_ready:
                 copy.wait_recv()
-        one, two, three = step + 1, step + 2, step + 3
-        upper = halo_pair[outer, 0, 1]
-        lower = halo_pair[outer, 1, 0]
-        ghost[0] = advanced(
-            one, upper, halo[outer, 0], halo_side[outer, 0], ghost_links[0], halo_pair[outer, 0, 0], x[one, 0]
-        )
-        ghost[1] = advanced(
-            one, lower, halo[outer, 1], halo_side[outer, 1], ghost_links[1], x[one, last], halo_pair[outer, 1, 1]
-        )
-        sweep_row(one, 0, upper, x[one, 1])
-        sweep_row(one, last, x[one, last - 1], lower)
-        sweep_row(two, 0, ghost[0], x[two, 1])
-        sweep_row(two, last, x[two, last - 1], ghost[1])
+        ghost_upper = add_flow(one, halo_part[outer, 0], ghost_links[0], x[one, 0])
+        ghost_lower = add_flow(one, halo_part[outer, 1], ghost_links[1], x[one, last])
+        x[two, 0] = add_flow(one, part[outer, 1], links[2, 0], halo_next[outer, 0])
+        x[two, last] = add_flow(one, part[outer, 0], links[3, last], halo_next[outer, 1])
+        x[three, last] = swept(two, last, x[two, last - 1], ghost_lower)
+        x[three, 0] = swept(two, 0, ghost_upper, x[two, 1])
         if final:
             send_out(0)
             send_out(last)
         else:
             halos = send_halo(outer + 1)
-        sweep_row(two, 1, x[two, 0], x[two, 2])
-        sweep_row(two, last - 1, x[two, last - 2], x[two, last])
+        x[three, 1] = add_flow(two, x[three, 1], links[2, 1], x[two, 0])
+        x[three, last - 1] = add_flow(two, x[three, last - 1], links[3, last - 1], x[two, last])
         if final:
             send_out(1)
             send_out(last - 1)
@@ -399,7 +397,7 @@
 
     out = pl.pallas_call(
         functools.partial(kernel, rows, blocks),
-        out_shape=jax.ShapeDtypeStruct((groups, blocks, SUB, LANES), f32),
+        out_shape=pltpu.VMEM((groups, blocks, SUB, LANES), f32),
         in_specs=[pl.BlockSpec(memory_space=pltpu.SMEM)] + [pl.BlockSpec(memory_space=pl.ANY)] * 5,
         out_specs=pl.BlockSpec(memory_space=pl.ANY),
         scratch_shapes=[
@@ -410,11 +408,11 @@
             vmem((OUTER, *grid), f32),
             vmem(grid, f32),
             vmem(row, f32),
-            vmem((2, 4, *row), f32),
+            vmem((2, *row), f32),
             vmem((OUTER, 2, *row), f32),
-            vmem((OUTER, 2, 2, *row), f32),
             vmem((OUTER, 2, *row), f32),
-            vmem((2, *row), f32),
+            vmem((OUTER, 2, *row), f32),
+            vmem((OUTER, 2, *row), f32),
             vmem(row, i32),
             vmem(row, i32),
             vmem(row, i32),

time: 39.5 us -> 36.2 us (0.916)
  the two profiles are of different devices: /device:TPU:4 before, /device:TPU:6 now
where the time goes in v3:
time: 36.2 us; the launch traced here: 35.9 us
  Pallas kernels  35.1 us (97%)
  local copies, waits for them, and re-layouts  0.8 us (2%)
    pallas_call x1, Pallas kernels, local(): pl.pallas_call(functools.partial(kernel, rows, blocks), out_shape=pltpu.V...  35.1 us
    unnamed x1, local copies, waits for them, and re-layouts  0.8 us

profile of v3, /device:TPU:6, one launch (start us, length us, event | category | flops | bytes accessed | tf_op | source)
XLA Modules:
  0.0 35.9 jit_solution(3055144438769613456)
XLA Ops:
  0.0 35.1 %shard_map.64 = f32[2,64,8,128]{3,2,1,0:T(8,128)S(1)} custom-call(f32[1,16]{1,0:T(1,128)} %table.1, s32[2,2,64,8,128]{4,3,2,1,0:T(8,128)} %bitcast.15, f32[2,64,8,128]{3,2,1,0:T(8,128)} %bitcast.16, f32[2,64,8,128]{3,2,1,0:T(8,128)} %bitcast.17, s32[64,128]{1,0:T(8,128)} %bitcast.18, s32[64,128]{1,0:T(8,128)} %bitcast.19), custom_call_target="tpu_custom_call" | custom-call | tf_op jit(solution)/shard_map/pallas_call | solution.py:398
  35.1 0.8 %copy.8 = f32[1,16,8192]{2,1,0:T(8,128)} copy(f32[1,16,8192]{2,1,0:T(8,128)S(1)} %bitcast.14) | data formatting | bytes 1048576

commit v4 on v3

--- a/solution.py
+++ b/solution.py
@@ -182,14 +182,11 @@
 
     def look_up_row(r, _):
         links[0, r] = jnp.where(at_end, zero, look_up(cls[0, r]))
-
-        @pl.when(r < last)
-        def _():
-            down_links[r] = look_up(cls[1, r])
-
+        down_links[r] = look_up(cls[1, r])
         return 0
 
-    lax.fori_loop(0, rows, look_up_row, 0)
+    lax.fori_loop(0, last, look_up_row, 0, unroll=3)
+    links[0, last] = jnp.where(at_end, zero, look_up(cls[0, last]))
 
     cells_up.wait_recv()
     picked[1] = pick(0, low_cells[...], jnp.zeros(row_shape, f32), 0, rows)
@@ -230,7 +227,7 @@
         coefficients(r, down_links[r - 1], down_links[r])
         return 0
 
-    lax.fori_loop(1, rows, coefficients_row, 0)
+    lax.fori_loop(1, rows, coefficients_row, 0, unroll=3)
     links_down.wait_recv()
     coefficients(0, links_in[...], down_links[0])
     scale[2] = scale[2] * scale[0]
@@ -290,7 +287,7 @@
 
         base_row(step, 0, None, x[step, 1])
         base_row(step, last, x[step, last - 1], None)
-        lax.fori_loop(1, last, base, 0)
+        lax.fori_loop(1, last, base, 0, unroll=2)
 
         volts_up.wait_recv()
         volts_down.wait_recv()
@@ -326,9 +323,9 @@
                 send_out(r)
             return 0
 
-        lax.fori_loop(2, last - 1, finish, 0)
-        lax.fori_loop(1, last, second, 0)
-        lax.fori_loop(2, last - 1, third, 0)
+        lax.fori_loop(2, last - 1, finish, 0, unroll=2)
+        lax.fori_loop(1, last, second, 0, unroll=2)
+        lax.fori_loop(2, last - 1, third, 0, unroll=2)
         x[three, 1] = swept(two, 1, None, x[two, 2])
         x[three, last - 1] = swept(two, last - 1, x[two, last - 2], None)
         if not final:

time: 36.2 us -> 35.6 us (0.983)
  Pallas kernels: 35.1 us -> 34.5 us
    pallas_call x1, Pallas kernels: 35.1 us -> 34.5 us  [local(): pl.pallas_call(functools.partial(kernel, rows, blocks), out_shape=pltpu.V...]
where the time goes in v4:
time: 35.6 us; the launch traced here: 35.3 us
  Pallas kernels  34.5 us (97%)
  local copies, waits for them, and re-layouts  0.8 us (2%)
    pallas_call x1, Pallas kernels, local(): pl.pallas_call(functools.partial(kernel, rows, blocks), out_shape=pltpu.V...  34.5 us
    unnamed x1, local copies, waits for them, and re-layouts  0.8 us

profile of v4, /device:TPU:6, one launch (start us, length us, event | category | flops | bytes accessed | tf_op | source)
XLA Modules:
  0.0 35.3 jit_solution(4737707953471066093)
XLA Ops:
  0.0 34.5 %shard_map.64 = f32[2,64,8,128]{3,2,1,0:T(8,128)S(1)} custom-call(f32[1,16]{1,0:T(1,128)} %table.1, s32[2,2,64,8,128]{4,3,2,1,0:T(8,128)} %bitcast.15, f32[2,64,8,128]{3,2,1,0:T(8,128)} %bitcast.16, f32[2,64,8,128]{3,2,1,0:T(8,128)} %bitcast.17, s32[64,128]{1,0:T(8,128)} %bitcast.18, s32[64,128]{1,0:T(8,128)} %bitcast.19), custom_call_target="tpu_custom_call" | custom-call | tf_op jit(solution)/shard_map/pallas_call | solution.py:395
  34.5 0.8 %copy.8 = f32[1,16,8192]{2,1,0:T(8,128)} copy(f32[1,16,8192]{2,1,0:T(8,128)S(1)} %bitcast.14) | data formatting | bytes 1048576

commit v5 on v4

--- a/solution.py
+++ b/solution.py
@@ -293,17 +293,17 @@
         volts_down.wait_recv()
         scale[0] = scale[2] * jnp.where(layer == layers - 1, f32(1.0), above[outer])
         scale[1] = scale[3] * below[outer]
-        finish_row(step, 1, None)
-        finish_row(step, last - 1, None)
+        one, two, three = step + 1, step + 2, step + 3
         halos[0].wait_recv()
         finish_row(step, 0, links[2, 0] * halo[outer, 0])
         halos[1].wait_recv()
         finish_row(step, last, links[3, last] * halo[outer, 1])
-        one, two, three = step + 1, step + 2, step + 3
         edges = [
             remote(x.at[one, last], halo_next.at[outer, 0], next_tile),
             remote(x.at[one, 0], halo_next.at[outer, 1], prev_tile),
         ]
+        finish_row(step, 1, None)
+        finish_row(step, last - 1, None)
         part[outer, 0] = swept(one, last, x[one, last - 1], None)
         edges.append(remote(part.at[outer, 0], halo_part.at[outer, 0], next_tile))
         part[outer, 1] = swept(one, 0, None, x[one, 1])
@@ -334,36 +334,38 @@
                     step + 3, cells[...], jnp.zeros(row_shape, f32), 2, last - 1
                 )
 
-        for copy in edges:
+        for copy in edges[:2]:
             copy.wait_recv()
+        x[two, 0] = add_flow(one, part[outer, 1], links[2, 0], halo_next[outer, 0])
+        x[two, last] = add_flow(one, part[outer, 0], links[3, last], halo_next[outer, 1])
+        x[three, last] = swept(two, last, x[two, last - 1], None)
+        x[three, 0] = swept(two, 0, None, x[two, 1])
+        for r, k, edge in ((1, 2, 0), (last - 1, 3, last)):
+            x[three, r] = add_flow(two, x[three, r], links[k, r], x[two, edge])
+            if final:
+                send_out(r)
+            else:
+                for slot, cells in ((2 * outer + 2, own_cells), (2 * outer + 3, low_cells)):
+                    picked[slot] = jnp.where(cells[...] == r, x[three, r], picked[slot])
         if outer == 0:
             for copy in ghosts_ready:
                 copy.wait_recv()
+        for copy in edges[2:]:
+            copy.wait_recv()
         ghost_upper = add_flow(one, halo_part[outer, 0], ghost_links[0], x[one, 0])
         ghost_lower = add_flow(one, halo_part[outer, 1], ghost_links[1], x[one, last])
-        x[two, 0] = add_flow(one, part[outer, 1], links[2, 0], halo_next[outer, 0])
-        x[two, last] = add_flow(one, part[outer, 0], links[3, last], halo_next[outer, 1])
-        x[three, last] = swept(two, last, x[two, last - 1], ghost_lower)
-        x[three, 0] = swept(two, 0, ghost_upper, x[two, 1])
+        x[three, 0] = add_flow(two, x[three, 0], links[2, 0], ghost_upper)
+        x[three, last] = add_flow(two, x[three, last], links[3, last], ghost_lower)
         if final:
             send_out(0)
             send_out(last)
         else:
             halos = send_halo(outer + 1)
-        x[three, 1] = add_flow(two, x[three, 1], links[2, 1], x[two, 0])
-        x[three, last - 1] = add_flow(two, x[three, last - 1], links[3, last - 1], x[two, last])
-        if final:
-            send_out(1)
-            send_out(last - 1)
-        else:
-            for k, cells in enumerate((own_cells, low_cells)):
-                slot = 2 * outer + 2 + k
-                acc = pick(three, cells[...], picked[slot], 0, 2)
-                picked[slot] = pick(three, cells[...], acc, last - 1, rows)
-                if k == 0:
-                    volts_up = remote(picked.at[slot], below.at[outer + 1], next_layer)
-                else:
-                    volts_down = remote(picked.at[slot], above.at[outer + 1], prev_layer)
+            for slot, cells in ((2 * outer + 2, own_cells), (2 * outer + 3, low_cells)):
+                acc = jnp.where(cells[...] == 0, x[three, 0], picked[slot])
+                picked[slot] = jnp.where(cells[...] == last, x[three, last], acc)
+            volts_up = remote(picked.at[2 * outer + 2], below.at[outer + 1], next_layer)
+            volts_down = remote(picked.at[2 * outer + 3], above.at[outer + 1], prev_layer)
 
     pltpu.make_async_copy(x.at[sweeps], x.at[sweeps], out_sem).wait()
     for copy in sent:

time: 35.6 us -> 35.2 us (0.989)
  no operation moved by 1% of the time
where the time goes in v5:
time: 35.2 us; the launch traced here: 35 us
  Pallas kernels  34.2 us (97%)
  local copies, waits for them, and re-layouts  0.8 us (2%)
    pallas_call x1, Pallas kernels, local(): pl.pallas_call(functools.partial(kernel, rows, blocks), out_shape=pltpu.V...  34.2 us
    unnamed x1, local copies, waits for them, and re-layouts  0.8 us

profile of v5, /device:TPU:6, one launch (start us, length us, event | category | flops | bytes accessed | tf_op | source)
XLA Modules:
  0.0 35.0 jit_solution(8653464859358183013)
XLA Ops:
  0.0 34.2 %shard_map.64 = f32[2,64,8,128]{3,2,1,0:T(8,128)S(1)} custom-call(f32[1,16]{1,0:T(1,128)} %table.1, s32[2,2,64,8,128]{4,3,2,1,0:T(8,128)} %bitcast.15, f32[2,64,8,128]{3,2,1,0:T(8,128)} %bitcast.16, f32[2,64,8,128]{3,2,1,0:T(8,128)} %bitcast.17, s32[64,128]{1,0:T(8,128)} %bitcast.18, s32[64,128]{1,0:T(8,128)} %bitcast.19), custom_call_target="tpu_custom_call" | custom-call | tf_op jit(solution)/shard_map/pallas_call | solution.py:397
  34.2 0.8 %copy.8 = f32[1,16,8192]{2,1,0:T(8,128)} copy(f32[1,16,8192]{2,1,0:T(8,128)S(1)} %bitcast.14) | data formatting | bytes 1048576

commit v6 on v5

--- a/solution.py
+++ b/solution.py
@@ -29,6 +29,27 @@
         terms.append((rho_next * rho_last, 2.0 * rho_next / half_width))
         rho_last = rho_next
     return terms
+
+
+def when(condition, action):
+    if condition is None:
+        action()
+    else:
+
+        @pl.when(condition)
+        def _():
+            action()
+
+
+class Message:
+    def __init__(self, copy, sends, receives):
+        self.copy, self.sends, self.receives = copy, sends, receives
+
+    def wait_recv(self):
+        when(self.receives, self.copy.wait_recv)
+
+    def wait_send(self):
+        when(self.sends, self.copy.wait_send)
 
 
 def kernel(
@@ -106,9 +127,21 @@
         ).start()
         return 0
 
+    has_prev = tile > 0
+    has_next = tile < tiles - 1
     barrier = pltpu.get_barrier_semaphore()
-    for peer in (next_layer, prev_layer, next_tile, prev_tile):
-        pl.semaphore_signal(barrier, inc=1, device_id=peer, device_id_type=MESH)
+    for peer, there in (
+        (next_layer, None),
+        (prev_layer, None),
+        (next_tile, has_next),
+        (prev_tile, has_prev),
+    ):
+        when(
+            there,
+            functools.partial(
+                pl.semaphore_signal, barrier, inc=1, device_id=peer, device_id_type=MESH
+            ),
+        )
 
     lax.fori_loop(0, rows, load_volts, 0)
     counts_in.start()
@@ -127,9 +160,14 @@
             device_id=peer,
             device_id_type=MESH,
         )
-        copy.start()
-        sent.append(copy)
-        return copy
+        sends, receives = None, None
+        if peer is next_tile:
+            sends, receives = has_next, has_prev
+        elif peer is prev_tile:
+            sends, receives = has_prev, has_next
+        when(sends, copy.start)
+        sent.append(Message(copy, sends, receives))
+        return sent[-1]
 
     lane = lax.broadcasted_iota(jnp.int32, row_shape, 1)
     block = lax.broadcasted_iota(jnp.int32, row_shape, 0)
@@ -156,6 +194,19 @@
             axis=0,
         )
 
+    def no_neighbour(side):
+        blank = jnp.zeros(row_shape, f32)
+        ghost_links[side] = blank
+        for outer in range(OUTER):
+            halo[outer, side] = blank
+            halo_next[outer, side] = blank
+            halo_part[outer, side] = blank
+        if side == 0:
+            links_in[...] = blank
+
+    when(jnp.logical_not(has_prev), lambda: no_neighbour(0))
+    when(jnp.logical_not(has_next), lambda: no_neighbour(1))
+
     cells_in.wait()
     counts_in.wait()
     pltpu.make_async_copy(x.at[1], x.at[0], in_sem.at[0]).wait()
@@ -163,7 +214,9 @@
     pltpu.make_async_copy(cls, cls, class_sem.at[0]).wait()
     down_links[last] = jnp.where(tile == tiles - 1, zero, look_up(cls[1, last]))
 
-    pl.semaphore_wait(barrier, 4)
+    inside = jnp.logical_and(has_prev, has_next)
+    when(inside, lambda: pl.semaphore_wait(barrier, 4))
+    when(jnp.logical_not(inside), lambda: pl.semaphore_wait(barrier, 3))
     cells_up = remote(own_cells, low_cells, next_layer)
     links_down = remote(down_links.at[last], links_in, next_tile)
     counts_up = remote(own_counts, low_counts, next_layer)

time: 35.2 us -> 35 us (level)
  the two profiles are of different devices: /device:TPU:6 before, /device:TPU:48 now
where the time goes in v6:
time: 35 us; the launch traced here: 34.8 us
  Pallas kernels  34 us (97%)
  local copies, waits for them, and re-layouts  0.8 us (2%)
    pallas_call x1, Pallas kernels, local(): pl.pallas_call(functools.partial(kernel, rows, blocks), out_shape=pltpu.V...  34 us
    unnamed x1, local copies, waits for them, and re-layouts  0.8 us

profile of v6, /device:TPU:48, one launch (start us, length us, event | category | flops | bytes accessed | tf_op | source)
XLA Modules:
  0.0 34.8 jit_solution(9418108037565335177)
XLA Ops:
  0.0 34.0 %shard_map.64 = f32[2,64,8,128]{3,2,1,0:T(8,128)S(1)} custom-call(f32[1,16]{1,0:T(1,128)} %table.1, s32[2,2,64,8,128]{4,3,2,1,0:T(8,128)} %bitcast.15, f32[2,64,8,128]{3,2,1,0:T(8,128)} %bitcast.16, f32[2,64,8,128]{3,2,1,0:T(8,128)} %bitcast.17, s32[64,128]{1,0:T(8,128)} %bitcast.18, s32[64,128]{1,0:T(8,128)} %bitcast.19), custom_call_target="tpu_custom_call" | custom-call | tf_op jit(solution)/shard_map/pallas_call | solution.py:450
  34.0 0.8 %copy.8 = f32[1,16,8192]{2,1,0:T(8,128)} copy(f32[1,16,8192]{2,1,0:T(8,128)S(1)} %bitcast.14) | data formatting | bytes 1048576

commit v7 on v6

--- a/solution.py
+++ b/solution.py
@@ -127,12 +127,14 @@
         ).start()
         return 0
 
+    has_lower = layer > 0
+    has_upper = layer < layers - 1
     has_prev = tile > 0
     has_next = tile < tiles - 1
     barrier = pltpu.get_barrier_semaphore()
     for peer, there in (
-        (next_layer, None),
-        (prev_layer, None),
+        (next_layer, has_upper),
+        (prev_layer, has_lower),
         (next_tile, has_next),
         (prev_tile, has_prev),
     ):
@@ -165,6 +167,10 @@
             sends, receives = has_next, has_prev
         elif peer is prev_tile:
             sends, receives = has_prev, has_next
+        elif peer is next_layer:
+            sends, receives = has_upper, has_lower
+        elif peer is prev_layer:
+            sends, receives = has_lower, has_upper
         when(sends, copy.start)
         sent.append(Message(copy, sends, receives))
         return sent[-1]
@@ -204,6 +210,18 @@
         if side == 0:
             links_in[...] = blank
 
+    def no_lower():
+        low_cells[...] = jnp.zeros(row_shape, jnp.int32)
+        low_counts[...] = jnp.zeros(row_shape, jnp.int32)
+        for outer in range(OUTER):
+            below[outer] = jnp.zeros(row_shape, f32)
+
+    def no_upper():
+        for outer in range(OUTER):
+            above[outer] = jnp.zeros(row_shape, f32)
+
+    when(jnp.logical_not(has_lower), no_lower)
+    when(jnp.logical_not(has_upper), no_upper)
     when(jnp.logical_not(has_prev), lambda: no_neighbour(0))
     when(jnp.logical_not(has_next), lambda: no_neighbour(1))
 
@@ -214,9 +232,14 @@
     pltpu.make_async_copy(cls, cls, class_sem.at[0]).wait()
     down_links[last] = jnp.where(tile == tiles - 1, zero, look_up(cls[1, last]))
 
-    inside = jnp.logical_and(has_prev, has_next)
-    when(inside, lambda: pl.semaphore_wait(barrier, 4))
-    when(jnp.logical_not(inside), lambda: pl.semaphore_wait(barrier, 3))
+    in_strips = jnp.logical_and(has_prev, has_next)
+    in_layers = jnp.logical_and(has_lower, has_upper)
+    for strips, strip_peers in ((in_strips, 2), (jnp.logical_not(in_strips), 1)):
+        for inner, layer_peers in ((in_layers, 2), (jnp.logical_not(in_layers), 1)):
+            when(
+                jnp.logical_and(strips, inner),
+                functools.partial(pl.semaphore_wait, barrier, strip_peers + layer_peers),
+            )
     cells_up = remote(own_cells, low_cells, next_layer)
     links_down = remote(down_links.at[last], links_in, next_tile)
     counts_up = remote(own_counts, low_counts, next_layer)

time: 35 us -> 32.1 us (0.917)
  the two profiles are of different devices: /device:TPU:48 before, /device:TPU:50 now
where the time goes in v7:
time: 32.1 us; the launch traced here: 31.8 us
  Pallas kernels  31 us (97%)
  local copies, waits for them, and re-layouts  0.8 us (2%)
    pallas_call x1, Pallas kernels, local(): pl.pallas_call(functools.partial(kernel, rows, blocks), out_shape=pltpu.V...  31 us
    unnamed x1, local copies, waits for them, and re-layouts  0.8 us

profile of v7, /device:TPU:50, one launch (start us, length us, event | category | flops | bytes accessed | tf_op | source)
XLA Modules:
  0.0 31.8 jit_solution(14814627091467504837)
XLA Ops:
  0.0 31.0 %shard_map.64 = f32[2,64,8,128]{3,2,1,0:T(8,128)S(1)} custom-call(f32[1,16]{1,0:T(1,128)} %table.1, s32[2,2,64,8,128]{4,3,2,1,0:T(8,128)} %bitcast.15, f32[2,64,8,128]{3,2,1,0:T(8,128)} %bitcast.16, f32[2,64,8,128]{3,2,1,0:T(8,128)} %bitcast.17, s32[64,128]{1,0:T(8,128)} %bitcast.18, s32[64,128]{1,0:T(8,128)} %bitcast.19), custom_call_target="tpu_custom_call" | custom-call | tf_op jit(solution)/shard_map/pallas_call | solution.py:473
  31.0 0.8 %copy.8 = f32[1,16,8192]{2,1,0:T(8,128)} copy(f32[1,16,8192]{2,1,0:T(8,128)S(1)} %bitcast.14) | data formatting | bytes 1048576
